TPU v7x, 32 devices: a whole 2x2x4 slice. The times are simulated.
32 devices in a mesh: ctx: 4 (over x, core), chan: 8 (over z, y).
Axes of the slice: x: 2, y: 2, z: 4, core: 2. Of those that a mesh axis runs over, the one named last changes fastest.
Arguments:
- proj: bfloat16 [3, 1024, 4096], P(None, 'chan', 'ctx'), may hold values from -6 to 6
- taps: bfloat16 [3, 64, 128], replicated, may hold values from -0.5 to 0.5
- rate: float32 [1024, 16], P('chan'), may hold values from 0.00012207031 to 0.0333333333
- residue: float32 [1024, 16], P('chan'), may hold values from -6 to 6
- skip: float32 [1024], P('chan'), may hold values from -6 to 6
- out_weight: bfloat16 [1024, 1024], replicated, may hold values from -0.1875 to 0.1875
Outputs:
- output: bfloat16 [1024, 4096], P('chan', 'ctx')
All inputs are finite; a program needn't handle non-finite values.
Results may differ from a plain program's by a relative error of at most 0.005.
Values may be sent and summed in bfloat16 or wider, within the bound.
A program may use at most 128 MiB of HBM per device.

v0:
```python
import functools
import jax
import jax.numpy as jnp
from jax import lax
from jax.experimental import pallas as pl
from jax.experimental.pallas import tpu as pltpu
from jax.sharding import PartitionSpec as P

GROUP = 16
BLOCK = 128


def lane_block(shape):
    return lax.broadcasted_iota(jnp.int32, shape, len(shape) - 1) // GROUP


def short_kernel(blocks, proj_ref, halo_ref, taps_ref, rate_ref, query_ref, mixed_ref, state_ref):
    groups = proj_ref.shape[1] // GROUP
    modes = rate_ref.shape[0]
    start = lax.axis_index("chan") * groups
    all_groups = taps_ref.shape[1]
    pick = (
        lax.broadcasted_iota(jnp.int32, (groups, all_groups), 1)
        == lax.broadcasted_iota(jnp.int32, (groups, all_groups), 0) + start
    ).astype(jnp.float32).astype(jnp.bfloat16)
    flip = (
        lax.broadcasted_iota(jnp.int32, (BLOCK, 2 * BLOCK), 1)
        == BLOCK - lax.broadcasted_iota(jnp.int32, (BLOCK, 2 * BLOCK), 0)
    ).astype(jnp.float32).astype(jnp.bfloat16)
    rows = []
    for stream in range(3):
        own = jnp.dot(pick, taps_ref[stream], preferred_element_type=jnp.float32)
        rows.append(
            jnp.dot(own.astype(jnp.bfloat16), flip, preferred_element_type=jnp.float32)
        )
    for g in range(groups):
        chans = slice(g * GROUP, (g + 1) * GROUP)
        outs = []
        for stream in range(3):
            wide = jnp.broadcast_to(rows[stream][g : g + 1, :], (BLOCK, 2 * BLOCK))
            band = pltpu.roll(wide, 0, 1, stride=1, stride_axis=0).astype(jnp.bfloat16)
            tiles = [
                proj_ref[stream, chans, b * BLOCK : (b + 1) * BLOCK] for b in range(blocks)
            ]
            now = jnp.concatenate(tiles, axis=0)
            before = jnp.concatenate([halo_ref[stream, chans, :]] + tiles[:-1], axis=0)
            signal = jnp.concatenate([before, now], axis=1)
            outs.append(
                lax.dot_general(
                    band, signal, (((1,), (1,)), ((), ())), preferred_element_type=jnp.float32
                )
            )
        query_ref[pl.ds(g, BLOCK, stride=groups), :] = outs[0]
        mixed_ref[pl.ds(g, BLOCK, stride=groups), :] = outs[1] * outs[2]
    decay = [jnp.exp(-rate_ref[m]) for m in range(modes)]

    def step(r, states):
        x = mixed_ref[pl.ds(pl.multiple_of(r * groups, groups), groups), :]
        return tuple(d * s + x for d, s in zip(decay, states))

    zero = jnp.zeros((groups, blocks * GROUP), jnp.float32)
    ends = lax.fori_loop(0, BLOCK, step, (zero,) * modes, unroll=8)
    at = lane_block(zero.shape)
    for m in range(modes):
        total, hop = ends[m], 1
        while hop < blocks:
            moved = jnp.exp(rate_ref[m] * (-float(BLOCK * hop))) * pltpu.roll(
                total, GROUP * hop, 1
            )
            total = total + jnp.where(at >= hop, moved, 0.0)
            hop *= 2
        state_ref[m] = total


def long_kernel(
    blocks, ctx, query_ref, mixed_ref, state_ref, ends_ref, rate_ref, residue_ref, skip_ref, gated_ref, work
):
    modes, groups = rate_ref.shape[0], rate_ref.shape[1]
    tokens = blocks * BLOCK
    index = lax.axis_index("ctx")
    shape = rate_ref.shape[1:]
    at = lane_block(shape)
    at_tokens = at.astype(jnp.float32) * float(BLOCK)
    entry, decay, weight = [], [], []
    for m in range(modes):
        rate = rate_ref[m]
        per_device = jnp.exp(rate * (-float(tokens)))
        incoming = jnp.zeros(shape, jnp.float32)
        for k in range(ctx):
            incoming = jnp.where(k < index, per_device * incoming + ends_ref[k, m], incoming)
        own = jnp.where(at >= 1, pltpu.roll(state_ref[m], GROUP, 1), 0.0)
        entry.append(own + jnp.exp(-rate * at_tokens) * incoming)
        decay.append(jnp.exp(-rate))
        weight.append(residue_ref[m] * jnp.sqrt(2.0 * rate / modes))
    skip = skip_ref[...]

    def step(r, states):
        where = pl.ds(pl.multiple_of(r * groups, groups), groups)
        x = mixed_ref[where, :]
        new = tuple(d * s + x for d, s in zip(decay, states))
        parts = [w * s for w, s in zip(weight, new)] + [skip * x]
        while len(parts) > 1:
            parts = [a + b for a, b in zip(parts[::2], parts[1::2])] + (
                [parts[-1]] if len(parts) % 2 else []
            )
        work[where, :] = query_ref[where, :] * parts[0]
        return new

    lax.fori_loop(0, BLOCK, step, tuple(entry), unroll=4)
    for g in range(groups):
        turned = work[pl.ds(g, BLOCK, stride=groups), :].T.astype(jnp.bfloat16)
        for b in range(blocks):
            gated_ref[g * GROUP : (g + 1) * GROUP, b * BLOCK : (b + 1) * BLOCK] = turned[
                b * GROUP : (b + 1) * GROUP
            ]


def per_device(ctx, proj, taps, rate, residue, skip, out_weight):
    width, tokens = proj.shape[1:]
    modes = rate.shape[1]
    groups, blocks = width // GROUP, tokens // BLOCK
    lanes = blocks * GROUP
    halo = lax.ppermute(
        proj[:, :, tokens - BLOCK :], "ctx", [(i, i + 1) for i in range(ctx - 1)]
    )

    def spread(value):
        return jnp.tile(value.reshape(groups, GROUP, modes).transpose(2, 0, 1), (1, 1, blocks))

    rate_l, residue_l = spread(rate), spread(residue)
    skip_l = jnp.tile(skip.reshape(groups, GROUP), (1, blocks))
    vmem = pl.BlockSpec(memory_space=pltpu.VMEM)
    major = jax.ShapeDtypeStruct((BLOCK * groups, lanes), jnp.float32)
    query, mixed, state = pl.pallas_call(
        functools.partial(short_kernel, blocks),
        out_shape=(major, major, jax.ShapeDtypeStruct((modes, groups, lanes), jnp.float32)),
        in_specs=[vmem] * 4,
        out_specs=(vmem,) * 3,
        compiler_params=pltpu.CompilerParams(vmem_limit_bytes=24 << 20),
        name="short",
    )(proj, halo, taps, rate_l)
    ends = lax.all_gather(state[:, :, lanes - GROUP :], "ctx")
    ends = jnp.tile(ends, (1, 1, 1, blocks))
    gated = pl.pallas_call(
        functools.partial(long_kernel, blocks, ctx),
        out_shape=jax.ShapeDtypeStruct((width, tokens), jnp.bfloat16),
        in_specs=[vmem] * 7,
        out_specs=vmem,
        scratch_shapes=[pltpu.VMEM(major.shape, jnp.float32)],
        compiler_params=pltpu.CompilerParams(vmem_limit_bytes=24 << 20),
        name="long",
    )(query, mixed, state, ends, rate_l, residue_l, skip_l)
    every = lax.all_gather(gated, "chan", axis=0, tiled=True)
    own = lax.dynamic_slice_in_dim(out_weight, lax.axis_index("chan") * width, width, 1)
    result = lax.dot_general(
        own, every, (((0,), (0,)), ((), ())), preferred_element_type=jnp.float32
    )
    return result.astype(jnp.bfloat16)


def solution(mesh):
    in_specs = (P(None, "chan", "ctx"), P(), P("chan", None), P("chan", None), P("chan"), P())
    out_specs = P("chan", "ctx")
    return jax.shard_map(
        functools.partial(per_device, mesh.shape["ctx"]),
        mesh=mesh,
        in_specs=in_specs,
        out_specs=out_specs,
        check_vma=False,
    )
```

profile of v0, /device:TPU:0, one launch (start us, length us, event | category | flops | bytes accessed | tf_op | source)
XLA Modules:
  0.0 95.0 jit_solution(10340337470438277536)
XLA Ops:
  6.5 0.0 copy-start
  6.5 0.0 copy-start.1
  6.5 0.0 copy-start.9
  6.5 0.0 all-gather.3.cloned.1.call-start
  6.5 1.1 %slice.6 = bf16[3,128,128]{2,1,0:T(8,128)(2,1)S(1)} slice(bf16[3,128,1024]{2,1,0:T(8,128)(2,1)} %proj_ref.1), slice={[0:3], [0:128], [896:1024]} | slice | bytes 196608 | tf_op jit(solution)/shard_map/slice | solution.py:124
  7.6 2.4 %collective-permute-start = (bf16[3,128,128]{2,1,0:T(8,128)(2,1)S(1)}, bf16[3,128,128]{2,1,0:T(8,128)(2,1)S(1)}, u32[]{:S(2)}, u32[]{:S(2)}) collective-permute-start(bf16[3,128,128]{2,1,0:T(8,128)(2,1)S(1)} %slice.6), channel_id=1, source_target_pairs={{0,8},{8,16},{16,24},{1,9},{9,17},{17,25},{2,10},{10,18},{18,26},{... | collective-permute-start | bytes 294920 | tf_op jit(solution)/shard_map/ppermute | solution.py:123
  10.0 0.8 reshape.22
  10.8 0.8 tile.18
  11.6 1.2 %tile.38.rate_ref = f32[16,8,128]{2,1,0:T(8,128)S(1)} reshape(f32[16,8,8,16]{3,2,1,0:T(8,128)} %tile.18) | data formatting | bytes 131072 | tf_op jit(solution)/shard_map/tile | solution.py:128
  12.8 0.8 reshape.23
  13.6 0.8 tile.41
  14.5 1.2 %tile.42.residue_ref = f32[16,8,128]{2,1,0:T(8,128)S(1)} reshape(f32[16,8,8,16]{3,2,1,0:T(8,128)} %tile.41) | data formatting | bytes 131072 | tf_op jit(solution)/shard_map/tile | solution.py:128
  15.7 0.0 copy-done.9
  15.7 0.1 tile.43
  15.8 0.1 tile.45.skip_ref
  15.9 0.0 collective-permute-done.halo_ref
  15.9 0.0 copy-start.6
  15.9 0.6 copy-done.6
  16.5 0.0 copy-done.1
  16.5 0.0 copy-start.7
  16.5 0.9 copy-done.7
  17.4 0.0 copy-start.8
  17.4 0.8 copy-done.8
  18.2 1.8 %short.1 = (f32[1024,128]{1,0:T(8,128)S(1)}, f32[1024,128]{1,0:T(8,128)S(1)}, f32[16,8,128]{2,1,0:T(8,128)S(1)}) custom-call(bf16[3,128,1024]{2,1,0:T(8,128)(2,1)S(1)} %copy-done.1, bf16[3,128,128]{2,1,0:T(8,128)(2,1)S(1)} %copy-done.7, bf16[3,64,128]{2,1,0:T(8,128)(2,1)S(1)} %copy-done.8, f32[16,8,128]{2,1,0:T(8,128)S(1)} %tile.38.rate_ref), custom_call_target="tpu_custom_call" | custom-call | tf_op jit(solution)/shard_map/short/pallas_call | solution.py:134
  20.0 0.0 copy-start.2
  20.0 0.8 copy-done.2
  20.8 0.0 copy-start.4
  20.8 0.1 slice.7
  20.9 7.1 %all-gather = f32[64,8,16]{2,1,0:T(8,128)S(1)} all-gather(f32[16,8,16]{2,1,0:T(8,128)S(1)} %slice.7), channel_id=2, replica_groups=mesh['ctx'=4,'chan'=8] {'ctx'}, dimensions={0}, use_global_device_ids=true | all-gather | bytes 40960 | tf_op jit(solution)/shard_map/all_gather | solution.py:142
  27.9 0.0 copy-done.4
  27.9 0.0 copy-start.3
  27.9 1.6 %tile.39 = f32[4,16,8,8,16]{4,3,2,1,0:T(8,128)} broadcast(f32[4,16,8,16]{3,2,1,0:T(8,128)S(1)} %bitcast.14), dimensions={0,1,2,4} | broadcast | bytes 294912 | tf_op jit(solution)/shard_map/tile | solution.py:143
  29.6 2.2 %tile.40.ends_ref = f32[4,16,8,128]{3,2,1,0:T(8,128)S(1)} reshape(f32[4,16,8,8,16]{4,3,2,1,0:T(8,128)} %tile.39) | data formatting | bytes 524288 | tf_op jit(solution)/shard_map/tile | solution.py:143
  31.7 0.0 copy-done.3
  31.7 0.0 copy-start.5
  31.8 0.8 copy-done.5
  32.6 2.2 %long.1 = bf16[128,1024]{1,0:T(8,128)(2,1)} custom-call(f32[1024,128]{1,0:T(8,128)S(1)} %get-tuple-element.8.query_ref, f32[1024,128]{1,0:T(8,128)S(1)} %copy-done.3, f32[16,8,128]{2,1,0:T(8,128)S(1)} %copy-done.5, f32[4,16,8,128]{3,2,1,0:T(8,128)S(1)} %tile.40.ends_ref, f32[16,8,128]{2,1,0:T(8,128)S(1)} %tile.38.rate_ref, ...), custom_call_target="tpu_custom_call" | custom-call | tf_op jit(solution)/shard_map/long/pallas_call | solution.py:144
  34.8 0.0 all-gather.3.cloned.1.call-update
  34.8 50.6 %all-gather.3.cloned.1.call-done = bf16[1024,1024]{1,0:T(8,128)(2,1)} async-done(((bf16[128,1024]{1,0:T(8,128)(2,1)}), bf16[1024,1024]{1,0:T(8,128)(2,1)}) %all-gather.3.cloned.1.call-update) | async-done | bytes 2097168 | tf_op jit(solution)/shard_map/all_gather | solution.py:153
  85.4 0.0 copy-done
  85.4 2.8 %convolution_convert_fusion = bf16[128,1024]{1,0:T(8,128)(2,1)} fusion(bf16[1024,1024]{1,0:T(8,128)(2,1)} %all-gather.3.cloned.1.call-done, bf16[1024,1024]{1,0:T(8,128)(2,1)S(1)} %copy-done, s32[]{:T(128)S(6)} %select_n.3), kind=kOutput, calls=%fused_computation | convolution fusion | flops 268566528 | bytes 2621444 | tf_op jit(solution)/shard_map/dot_general | solution.py:155
  (1 shorter events, 0.0 us)
Async XLA Ops:
  6.5 78.8 %copy-start = (bf16[1024,1024]{1,0:T(8,128)(2,1)S(1)}, bf16[1024,1024]{1,0:T(8,128)(2,1)}, u32[]{:S(2)}) copy-start(bf16[1024,1024]{1,0:T(8,128)(2,1)} %param.11) | copy-start | bytes 6291460
  6.5 10.0 %copy-start.1 = (bf16[3,128,1024]{2,1,0:T(8,128)(2,1)S(1)}, bf16[3,128,1024]{2,1,0:T(8,128)(2,1)}, u32[]{:S(2)}) copy-start(bf16[3,128,1024]{2,1,0:T(8,128)(2,1)} %proj_ref.1) | copy-start | bytes 2359300
  6.5 9.1 %copy-start.9 = (f32[128]{0:T(128)S(1)}, f32[128]{0:T(128)}, u32[]{:S(2)}) copy-start(f32[128]{0:T(128)} %param.10) | copy-start | bytes 1540
  6.5 78.8 %all-gather.3.cloned.1.call-start = ((), (), s32[]{:S(2)}) async-start(), calls=%async_computation | async-start | bytes 2359296 | tf_op jit(solution)/shard_map/all_gather | solution.py:153
  7.6 8.2 %collective-permute-start = (bf16[3,128,128]{2,1,0:T(8,128)(2,1)S(1)}, bf16[3,128,128]{2,1,0:T(8,128)(2,1)S(1)}, u32[]{:S(2)}, u32[]{:S(2)}) collective-permute-start(bf16[3,128,128]{2,1,0:T(8,128)(2,1)S(1)} %slice.6), channel_id=1, source_target_pairs={{0,8},{8,16},{16,24},{1,9},{9,17},{17,25},{2,10},{10,18},{18,26},{... | collective-permute-start | bytes 294920 | tf_op jit(solution)/shard_map/ppermute | solution.py:123
  15.9 0.6 copy-start.6
  16.5 0.9 copy-start.7
  17.4 0.8 copy-start.8
  20.0 0.8 copy-start.2
  20.8 7.1 %copy-start.4 = (f32[16,8,128]{2,1,0:T(8,128)}, f32[16,8,128]{2,1,0:T(8,128)S(1)}, u32[]{:S(2)}) copy-start(f32[16,8,128]{2,1,0:T(8,128)S(1)} %get-tuple-element.10.state_ref) | copy-start | bytes 196612
  27.9 3.8 %copy-start.3 = (f32[1024,128]{1,0:T(8,128)S(1)}, f32[1024,128]{1,0:T(8,128)}, u32[]{:S(2)}) copy-start(f32[1024,128]{1,0:T(8,128)} %copy-done.2) | copy-start | bytes 1572868
  31.7 0.8 copy-start.5
Sparse Core Ops, SparseCore 0:
  34.9 50.3 all-gather.2
where the time goes:
time: 95.5 us; the launch traced here: 95 us
  waiting for transfers between devices  50.6 us (53%)
  local copies, waits for them, and re-layouts  14.8 us (15%)
  between operations  13.5 us (14%)
  blocking collectives  7.07 us (7%)
  Pallas kernels  3.99 us (4%)
  matrix products  2.78 us (3%)
  starting transfers between devices  2.35 us (2%)
    all_gather x1, waiting for transfers between devices, per_device(): every = lax.all_gather(gated, 'chan', axis=0, tiled=True)  50.6 us
    all_gather x1, blocking collectives, per_device(): ends = lax.all_gather(state[:, :, lanes - GROUP:], 'ctx')  7.07 us
    another operation x4, local copies, waits for them, and re-layouts, spread(): jnp.tile(value.reshape(groups, GROUP, modes).transpose(2, 0, 1), (1, 1, b...  4.15 us
    unnamed x20, local copies, waits for them, and re-layouts  3.97 us
    another operation x2, local copies, waits for them, and re-layouts, per_device(): ends = jnp.tile(ends, (1, 1, 1, blocks))  3.79 us
    dot_general x1, matrix products, per_device(): lax.dot_general(own, every, (((0,), (0,)), ((), ())), preferred_element_t...  2.78 us
    ppermute x1, starting transfers between devices, per_device(): lax.ppermute(proj[:, :, tokens - BLOCK:], 'ctx', [(i, i + 1) for i in ran...  2.35 us
    pallas_call x1, Pallas kernels, per_device(): pl.pallas_call(functools.partial(long_kernel, blocks, ctx), out_shape=jax...  2.21 us
  transfers between devices with their start and end apart: 2, of which 1 were waited for; matrix products, arithmetic and copies ran while one was open for 6% of the time, Pallas kernels for 0%

commit v1 on v0

v1 whole, which is shorter than its diff:
```python
import functools
import jax
import jax.numpy as jnp
from jax import lax
from jax.experimental import pallas as pl
from jax.experimental.pallas import tpu as pltpu
from jax.sharding import PartitionSpec as P

GROUP = 16
BLOCK = 128
PIECES = 4
MESH = pl.DeviceIdType.MESH
HIGHEST = lax.Precision.HIGHEST


def iota(shape, axis):
    return lax.broadcasted_iota(jnp.int32, shape, axis)


def one_hot(hit, dtype=jnp.float32):
    return hit.astype(jnp.float32).astype(dtype)


def ring_place(chan, n):
    row, side = chan // 2, chan % 2
    return row + side * (n - 1 - 2 * row)


def ring_chan(place, n):
    side = place // (n // 2)
    row = place + side * (n - 1 - 2 * place)
    return 2 * row + side


def fused(
    ctx,
    chans,
    proj_ref,
    taps_ref,
    rate_ref,
    residue_ref,
    skip_ref,
    weight_ref,
    out_ref,
    halo,
    query,
    mixed,
    work,
    bands,
    rate_s,
    residue_s,
    state,
    ends,
    own_weight,
    gath,
    acc,
    weight_sem,
    halo_sems,
    end_send,
    end_recv,
    ring_send,
    ring_recv,
):
    width, tokens = proj_ref.shape[1:]
    modes = rate_ref.shape[1]
    groups, blocks = width // GROUP, tokens // BLOCK
    lanes = blocks * GROUP
    cols = tokens // PIECES
    index = lax.axis_index("ctx")
    chan = lax.axis_index("chan")
    place = ring_place(chan, chans)
    right = ring_chan((place + 1) % chans, chans)
    left = ring_chan((place + chans - 1) % chans, chans)

    barrier = pltpu.get_barrier_semaphore()
    for hop in range(1, ctx):
        pl.semaphore_signal(
            barrier, inc=1, device_id={"ctx": (index + hop) % ctx}, device_id_type=MESH
        )
    for peer in (left, right):
        pl.semaphore_signal(barrier, inc=1, device_id={"chan": peer}, device_id_type=MESH)

    if weight_ref.shape[1] == width:
        weight_from = weight_ref
    else:
        weight_from = weight_ref.at[:, pl.ds(pl.multiple_of(chan * width, width), width)]
    weight_copy = pltpu.make_async_copy(weight_from, own_weight, weight_sem)
    weight_copy.start()

    pl.semaphore_wait(barrier, ctx + 1)
    halo_copy = pltpu.make_async_remote_copy(
        src_ref=proj_ref.at[:, :, pl.ds(tokens - BLOCK, BLOCK)],
        dst_ref=halo,
        send_sem=halo_sems.at[0],
        recv_sem=halo_sems.at[1],
        device_id={"ctx": (index + 1) % ctx},
        device_id_type=MESH,
    )

    @pl.when(index < ctx - 1)
    def _():
        halo_copy.start()

    all_groups = taps_ref.shape[1]
    pick = one_hot(
        iota((groups, all_groups), 1) == iota((groups, all_groups), 0) + chan * groups,
        jnp.bfloat16,
    )
    flip = one_hot(
        iota((BLOCK, 2 * BLOCK), 1) == BLOCK - iota((BLOCK, 2 * BLOCK), 0), jnp.bfloat16
    )
    for stream in range(3):
        own = jnp.dot(pick, taps_ref[stream], preferred_element_type=jnp.float32)
        rows = jnp.dot(own.astype(jnp.bfloat16), flip, preferred_element_type=jnp.float32)
        for g in range(groups):
            wide = jnp.broadcast_to(rows[g : g + 1, :], (BLOCK, 2 * BLOCK))
            bands[stream, g] = pltpu.roll(wide, 0, 1, stride=1, stride_axis=0).astype(
                jnp.bfloat16
            )

    high = modes * groups
    expand = one_hot(iota((high, modes), 0) // groups == iota((high, modes), 1))
    kept = iota((high, width), 1) // GROUP == iota((high, width), 0) % groups
    spread = one_hot(iota((width, lanes), 0) % GROUP == iota((width, lanes), 1) % GROUP)

    def spread_rows(value):
        tall = lax.dot_general(
            expand,
            value,
            (((1,), (1,)), ((), ())),
            precision=HIGHEST,
            preferred_element_type=jnp.float32,
        )
        return jnp.dot(
            jnp.where(kept, tall, 0.0),
            spread,
            precision=HIGHEST,
            preferred_element_type=jnp.float32,
        )

    rate_s[...] = spread_rows(rate_ref[...])
    residue_s[...] = spread_rows(residue_ref[...]) * jnp.sqrt(2.0 * rate_s[...] / modes)
    skip_rows = jnp.where(
        iota((groups, width), 1) // GROUP == iota((groups, width), 0),
        jnp.broadcast_to(skip_ref[...], (groups, width)),
        0.0,
    )
    skip = jnp.dot(skip_rows, spread, precision=HIGHEST, preferred_element_type=jnp.float32)

    def of_mode(ref, m):
        return ref[m * groups : (m + 1) * groups, :]

    decay = [jnp.exp(-of_mode(rate_s, m)) for m in range(modes)]

    @pl.when(index > 0)
    def _():
        halo_copy.wait_recv()

    @pl.when(index == 0)
    def _():
        halo[...] = jnp.zeros_like(halo)

    def short(stream, g):
        rows_of = slice(g * GROUP, (g + 1) * GROUP)
        tiles = [proj_ref[stream, rows_of, b * BLOCK : (b + 1) * BLOCK] for b in range(blocks)]
        before = [halo[stream, rows_of, :]] + tiles[:-1]
        signal = jnp.concatenate(
            [jnp.concatenate(before, axis=0), jnp.concatenate(tiles, axis=0)], axis=1
        )
        return lax.dot_general(
            bands[stream, g], signal, (((1,), (1,)), ((), ())), preferred_element_type=jnp.float32
        )

    for g in range(groups):
        mixed[pl.ds(g, BLOCK, stride=groups), :] = short(1, g) * short(2, g)

    def gather_step(r, states):
        x = mixed[pl.ds(pl.multiple_of(r * groups, groups), groups), :]
        return tuple(d * s + x for d, s in zip(decay, states))

    zero = jnp.zeros((groups, lanes), jnp.float32)
    last = lax.fori_loop(0, BLOCK, gather_step, (zero,) * modes, unroll=8)
    at = iota(zero.shape, 1) // GROUP
    for m in range(modes):
        total, hop = last[m], 1
        while hop < blocks:
            moved = jnp.exp(of_mode(rate_s, m) * (-float(BLOCK * hop))) * pltpu.roll(
                total, GROUP * hop, 1
            )
            total = total + jnp.where(at >= hop, moved, 0.0)
            hop *= 2
        state[m * groups : (m + 1) * groups, :] = total

    end_copies = [
        pltpu.make_async_remote_copy(
            src_ref=state,
            dst_ref=ends.at[hop - 1],
            send_sem=end_send.at[hop - 1],
            recv_sem=end_recv.at[hop - 1],
            device_id={"ctx": (index + hop) % ctx},
            device_id_type=MESH,
        )
        for hop in range(1, ctx)
    ]
    for hop in range(1, ctx):

        @pl.when(index < ctx - hop)
        def _():
            end_copies[hop - 1].start()

    for g in range(groups):
        query[pl.ds(g, BLOCK, stride=groups), :] = short(0, g)

    for hop in range(1, ctx):

        @pl.when(index >= hop)
        def _():
            end_copies[hop - 1].wait_recv()

        @pl.when(index < hop)
        def _():
            ends[hop - 1] = jnp.zeros((high, lanes), jnp.float32)

    at_tokens = at.astype(jnp.float32) * float(BLOCK)
    entry, weight = [], []
    for m in range(modes):
        rate = of_mode(rate_s, m)
        per_device = jnp.exp(rate * (-float(tokens)))
        incoming = jnp.zeros_like(zero)
        for hop in range(ctx - 1, 0, -1):
            incoming = per_device * incoming + ends[hop - 1, m * groups : (m + 1) * groups, :]
        incoming = jnp.where(at == blocks - 1, incoming, 0.0)
        hop = 1
        while hop < blocks:
            incoming = incoming + pltpu.roll(incoming, GROUP * hop, 1)
            hop *= 2
        own = jnp.where(at >= 1, pltpu.roll(of_mode(state, m), GROUP, 1), 0.0)
        entry.append(own + jnp.exp(-rate * at_tokens) * incoming)
        weight.append(of_mode(residue_s, m))

    def step(r, states):
        where = pl.ds(pl.multiple_of(r * groups, groups), groups)
        x = mixed[where, :]
        new = tuple(d * s + x for d, s in zip(decay, states))
        parts = [w * s for w, s in zip(weight, new)] + [skip * x]
        while len(parts) > 1:
            parts = [a + b for a, b in zip(parts[::2], parts[1::2])] + (
                [parts[-1]] if len(parts) % 2 else []
            )
        work[where, :] = query[where, :] * parts[0]
        return new

    lax.fori_loop(0, BLOCK, step, tuple(entry), unroll=4)
    per_piece = blocks // PIECES
    for g in range(groups):
        turned = work[pl.ds(g, BLOCK, stride=groups), :].T.astype(jnp.bfloat16)
        for b in range(blocks):
            inside = (b % per_piece) * BLOCK
            gath[
                chan, b // per_piece, g * GROUP : (g + 1) * GROUP, inside : inside + BLOCK
            ] = turned[b * GROUP : (b + 1) * GROUP]

    half = chans // 2

    def ring_copy(way, hop, piece):
        shard = ring_chan((place + chans + (-hop if way == 0 else hop)) % chans, chans)
        return pltpu.make_async_remote_copy(
            src_ref=gath.at[shard, piece],
            dst_ref=gath.at[shard, piece],
            send_sem=ring_send.at[way, hop, piece],
            recv_sem=ring_recv.at[way, hop, piece],
            device_id={"chan": right if way == 0 else left},
            device_id_type=MESH,
        )

    def travels(way, hop, piece):
        if hop < half - 1:
            return True
        return hop == half - 1 and (piece < PIECES // 2) == (way == 0)

    copies = {}
    for piece in range(PIECES):
        for way in range(2):
            copies[way, 0, piece] = ring_copy(way, 0, piece)
            copies[way, 0, piece].start()
    weight_copy.wait()

    def project(shard, piece):
        rows_of = pl.ds(pl.multiple_of(shard * width, width), width)
        return lax.dot_general(
            own_weight[rows_of, :],
            gath[shard, piece],
            (((0,), (0,)), ((), ())),
            preferred_element_type=jnp.float32,
        )

    for piece in range(PIECES):
        acc[piece] = project(chan, piece)
    for hop in range(1, half + 1):
        for piece in range(PIECES):
            arrived = []
            for way in range(2):
                if not travels(way, hop - 1, piece):
                    continue
                copies[way, hop - 1, piece].wait_recv()
                if travels(way, hop, piece):
                    copies[way, hop, piece] = ring_copy(way, hop, piece)
                    copies[way, hop, piece].start()
                arrived.append(
                    ring_chan((place + chans + (-hop if way == 0 else hop)) % chans, chans)
                )
            total = acc[piece]
            for shard in arrived:
                total = total + project(shard, piece)
            if hop == half:
                out_ref[:, piece * cols : (piece + 1) * cols] = total.astype(out_ref.dtype)
            else:
                acc[piece] = total

    for key in copies:
        copies[key].wait_send()

    @pl.when(index < ctx - 1)
    def _():
        halo_copy.wait_send()

    for hop in range(1, ctx):

        @pl.when(index < ctx - hop)
        def _():
            end_copies[hop - 1].wait_send()


def per_device(ctx, chans, proj, taps, rate, residue, skip, out_weight):
    width, tokens = proj.shape[1:]
    modes = rate.shape[1]
    groups, blocks = width // GROUP, tokens // BLOCK
    lanes = blocks * GROUP
    if width % 128:
        out_weight = lax.dynamic_slice_in_dim(
            out_weight, lax.axis_index("chan") * width, width, 1
        )
    vmem = pl.BlockSpec(memory_space=pltpu.VMEM)
    major = pltpu.VMEM((BLOCK * groups, lanes), jnp.float32)
    table = pltpu.VMEM((modes * groups, lanes), jnp.float32)
    return pl.pallas_call(
        functools.partial(fused, ctx, chans),
        out_shape=jax.ShapeDtypeStruct((width, tokens), jnp.bfloat16),
        in_specs=[vmem] * 5 + [pl.BlockSpec(memory_space=pl.ANY)],
        out_specs=vmem,
        scratch_shapes=[
            pltpu.VMEM((3, width, BLOCK), jnp.bfloat16),
            major,
            major,
            major,
            pltpu.VMEM((3, groups, BLOCK, 2 * BLOCK), jnp.bfloat16),
            table,
            table,
            table,
            pltpu.VMEM((ctx - 1, modes * groups, lanes), jnp.float32),
            pltpu.VMEM((chans * width, width), jnp.bfloat16),
            pltpu.VMEM((chans, PIECES, width, tokens // PIECES), jnp.bfloat16),
            pltpu.VMEM((PIECES, width, tokens // PIECES), jnp.float32),
            pltpu.SemaphoreType.DMA,
            pltpu.SemaphoreType.DMA((2,)),
            pltpu.SemaphoreType.DMA((ctx - 1,)),
            pltpu.SemaphoreType.DMA((ctx - 1,)),
            pltpu.SemaphoreType.DMA((2, chans // 2, PIECES)),
            pltpu.SemaphoreType.DMA((2, chans // 2, PIECES)),
        ],
        compiler_params=pltpu.CompilerParams(
            vmem_limit_bytes=32 << 20, collective_id=0, has_side_effects=True
        ),
        name="fused",
    )(proj, taps, rate, residue, skip.reshape(1, width), out_weight)


def solution(mesh):
    in_specs = (P(None, "chan", "ctx"), P(), P("chan", None), P("chan", None), P("chan"), P())
    out_specs = P("chan", "ctx")
    return jax.shard_map(
        functools.partial(per_device, mesh.shape["ctx"], mesh.shape["chan"]),
        mesh=mesh,
        in_specs=in_specs,
        out_specs=out_specs,
        check_vma=False,
    )
```

time: 95.5 us -> 40.8 us (0.43)
  the two profiles are of different devices: /device:TPU:0 before, /device:TPU:3 now
where the time goes in v1:
time: 40.8 us; the launch traced here: 40.2 us
  Pallas kernels  33.8 us (83%)
  local copies, waits for them, and re-layouts  6.47 us (16%)
    pallas_call x1, Pallas kernels, per_device(): pl.pallas_call(functools.partial(fused, ctx, chans), out_shape=jax.ShapeD...  33.8 us
    unnamed x11, local copies, waits for them, and re-layouts  6.47 us

profile of v1, /device:TPU:3, one launch (start us, length us, event | category | flops | bytes accessed | tf_op | source)
XLA Modules:
  0.0 40.2 jit_solution(5516712210567263330)
XLA Ops:
  0.0 0.8 %copy.7.rate_ref = f32[128,16]{1,0:T(8,128)S(1)} copy(f32[128,16]{0,1:T(8,128)} %param.8) | data formatting | bytes 16384 | tf_op args[2]
  0.8 0.8 %copy.8.residue_ref = f32[128,16]{1,0:T(8,128)S(1)} copy(f32[128,16]{0,1:T(8,128)} %param.9) | data formatting | bytes 16384 | tf_op args[3]
  1.6 0.0 copy-start
  1.6 1.6 %copy-done = bf16[1024,1024]{1,0:T(8,128)(2,1)S(1)} copy-done((bf16[1024,1024]{1,0:T(8,128)(2,1)S(1)}, bf16[1024,1024]{1,0:T(8,128)(2,1)}, u32[]{:S(2)}) %copy-start) | copy-done | bytes 2097176
  3.2 0.0 copy-start.1
  3.2 1.1 %copy-done.1 = bf16[3,128,1024]{2,1,0:T(8,128)(2,1)S(1)} copy-done((bf16[3,128,1024]{2,1,0:T(8,128)(2,1)S(1)}, bf16[3,128,1024]{2,1,0:T(8,128)(2,1)}, u32[]{:S(2)}) %copy-start.1) | copy-done | bytes 786456
  4.3 0.0 copy-start.2
  4.3 0.8 %copy-done.2 = bf16[3,64,128]{2,1,0:T(8,128)(2,1)S(1)} copy-done((bf16[3,64,128]{2,1,0:T(8,128)(2,1)S(1)}, bf16[3,64,128]{2,1,0:T(8,128)(2,1)}, u32[]{:S(2)}) %copy-start.2) | copy-done | bytes 49176
  5.1 0.0 copy-start.3
  5.1 0.7 %copy-done.3 = f32[128]{0:T(128)S(1)} copy-done((f32[128]{0:T(128)S(1)}, f32[128]{0:T(128)}, u32[]{:S(2)}) %copy-start.3) | copy-done | bytes 536
  5.8 33.8 %fused.1 = bf16[128,1024]{1,0:T(8,128)(2,1)S(1)} custom-call(bf16[3,128,1024]{2,1,0:T(8,128)(2,1)S(1)} %copy-done.1, bf16[3,64,128]{2,1,0:T(8,128)(2,1)S(1)} %copy-done.2, f32[128,16]{1,0:T(8,128)S(1)} %copy.7.rate_ref, f32[128,16]{1,0:T(8,128)S(1)} %copy.8.residue_ref, f32[1,128]{1,0:T(1,128)S(1)} %bitcast.1, bf16[1024,1024]{1,0:T(8,128)(2,1)S(1)} %copy-done), custom_call_target="tpu_custom_call" | custom-call | tf_op jit(solution)/shard_map/fused/pallas_call | solution.py:346
  39.5 0.7 %copy.10 = bf16[128,1024]{1,0:T(8,128)(2,1)} copy(bf16[128,1024]{1,0:T(8,128)(2,1)S(1)} %fused.1) | data formatting | bytes 524288
Async XLA Ops:
  1.6 1.6 %copy-start = (bf16[1024,1024]{1,0:T(8,128)(2,1)S(1)}, bf16[1024,1024]{1,0:T(8,128)(2,1)}, u32[]{:S(2)}) copy-start(bf16[1024,1024]{1,0:T(8,128)(2,1)} %weight_ref.1) | copy-start | bytes 6291460
  3.2 1.1 %copy-start.1 = (bf16[3,128,1024]{2,1,0:T(8,128)(2,1)S(1)}, bf16[3,128,1024]{2,1,0:T(8,128)(2,1)}, u32[]{:S(2)}) copy-start(bf16[3,128,1024]{2,1,0:T(8,128)(2,1)} %proj_ref.1) | copy-start | bytes 2359300
  4.3 0.8 %copy-start.2 = (bf16[3,64,128]{2,1,0:T(8,128)(2,1)S(1)}, bf16[3,64,128]{2,1,0:T(8,128)(2,1)}, u32[]{:S(2)}) copy-start(bf16[3,64,128]{2,1,0:T(8,128)(2,1)} %taps_ref.1) | copy-start | bytes 147460
  5.1 0.7 %copy-start.3 = (f32[128]{0:T(128)S(1)}, f32[128]{0:T(128)}, u32[]{:S(2)}) copy-start(f32[128]{0:T(128)} %param.10) | copy-start | bytes 1540

commit v2 on v1

--- a/solution.py
+++ b/solution.py
@@ -35,13 +35,18 @@
 def fused(
     ctx,
     chans,
+    proj_in,
+    taps_in,
+    rate_in,
+    residue_in,
+    skip_in,
+    weight_ref,
+    out_ref,
     proj_ref,
     taps_ref,
     rate_ref,
     residue_ref,
     skip_ref,
-    weight_ref,
-    out_ref,
     halo,
     query,
     mixed,
@@ -55,6 +60,7 @@
     gath,
     acc,
     weight_sem,
+    load_sems,
     halo_sems,
     end_send,
     end_recv,
@@ -62,7 +68,7 @@
     ring_recv,
 ):
     width, tokens = proj_ref.shape[1:]
-    modes = rate_ref.shape[1]
+    modes = rate_ref.shape[0]
     groups, blocks = width // GROUP, tokens // BLOCK
     lanes = blocks * GROUP
     cols = tokens // PIECES
@@ -80,6 +86,20 @@
     for peer in (left, right):
         pl.semaphore_signal(barrier, inc=1, device_id={"chan": peer}, device_id_type=MESH)
 
+    loads = [
+        pltpu.make_async_copy(source, target, load_sems.at[k])
+        for k, (source, target) in enumerate(
+            (
+                (taps_in, taps_ref),
+                (rate_in, rate_ref),
+                (residue_in, residue_ref),
+                (skip_in, skip_ref),
+                (proj_in, proj_ref),
+            )
+        )
+    ]
+    for load in loads:
+        load.start()
     if weight_ref.shape[1] == width:
         weight_from = weight_ref
     else:
@@ -89,7 +109,7 @@
 
     pl.semaphore_wait(barrier, ctx + 1)
     halo_copy = pltpu.make_async_remote_copy(
-        src_ref=proj_ref.at[:, :, pl.ds(tokens - BLOCK, BLOCK)],
+        src_ref=proj_in.at[:, :, pl.ds(tokens - BLOCK, BLOCK)],
         dst_ref=halo,
         send_sem=halo_sems.at[0],
         recv_sem=halo_sems.at[1],
@@ -101,6 +121,7 @@
     def _():
         halo_copy.start()
 
+    loads[0].wait()
     all_groups = taps_ref.shape[1]
     pick = one_hot(
         iota((groups, all_groups), 1) == iota((groups, all_groups), 0) + chan * groups,
@@ -118,6 +139,8 @@
                 jnp.bfloat16
             )
 
+    for load in loads[1:4]:
+        load.wait()
     high = modes * groups
     expand = one_hot(iota((high, modes), 0) // groups == iota((high, modes), 1))
     kept = iota((high, width), 1) // GROUP == iota((high, width), 0) % groups
@@ -127,7 +150,7 @@
         tall = lax.dot_general(
             expand,
             value,
-            (((1,), (1,)), ((), ())),
+            (((1,), (0,)), ((), ())),
             precision=HIGHEST,
             preferred_element_type=jnp.float32,
         )
@@ -151,6 +174,8 @@
         return ref[m * groups : (m + 1) * groups, :]
 
     decay = [jnp.exp(-of_mode(rate_s, m)) for m in range(modes)]
+
+    loads[4].wait()
 
     @pl.when(index > 0)
     def _():
@@ -346,9 +371,14 @@
     return pl.pallas_call(
         functools.partial(fused, ctx, chans),
         out_shape=jax.ShapeDtypeStruct((width, tokens), jnp.bfloat16),
-        in_specs=[vmem] * 5 + [pl.BlockSpec(memory_space=pl.ANY)],
+        in_specs=[pl.BlockSpec(memory_space=pltpu.HBM)] * 6,
         out_specs=vmem,
         scratch_shapes=[
+            pltpu.VMEM(proj.shape, proj.dtype),
+            pltpu.VMEM(taps.shape, taps.dtype),
+            pltpu.VMEM((modes, width), jnp.float32),
+            pltpu.VMEM((modes, width), jnp.float32),
+            pltpu.VMEM((1, width), jnp.float32),
             pltpu.VMEM((3, width, BLOCK), jnp.bfloat16),
             major,
             major,
@@ -362,6 +392,7 @@
             pltpu.VMEM((chans, PIECES, width, tokens // PIECES), jnp.bfloat16),
             pltpu.VMEM((PIECES, width, tokens // PIECES), jnp.float32),
             pltpu.SemaphoreType.DMA,
+            pltpu.SemaphoreType.DMA((5,)),
             pltpu.SemaphoreType.DMA((2,)),
             pltpu.SemaphoreType.DMA((ctx - 1,)),
             pltpu.SemaphoreType.DMA((ctx - 1,)),
@@ -369,10 +400,10 @@
             pltpu.SemaphoreType.DMA((2, chans // 2, PIECES)),
         ],
         compiler_params=pltpu.CompilerParams(
-            vmem_limit_bytes=32 << 20, collective_id=0, has_side_effects=True
+            vmem_limit_bytes=58 << 20, collective_id=0, has_side_effects=True
         ),
         name="fused",
-    )(proj, taps, rate, residue, skip.reshape(1, width), out_weight)
+    )(proj, taps, rate.T, residue.T, skip.reshape(1, width), out_weight)
 
 
 def solution(mesh):

time: 40.8 us -> 36.9 us (0.904)
  local copies, waits for them, and re-layouts: 6.47 us -> 1.67 us
  Pallas kernels: 33.8 us -> 35.1 us
    unnamed x11 -> x1, local copies, waits for them, and re-layouts: 6.47 us -> 1.67 us
    pallas_call x1, Pallas kernels: 33.8 us -> 35.1 us  [per_device(): pl.pallas_call(functools.partial(fused, ctx, chans), out_shape=jax.ShapeD...]
where the time goes in v2:
time: 36.9 us; the launch traced here: 36.7 us
  Pallas kernels  35.1 us (95%)
  local copies, waits for them, and re-layouts  1.67 us (5%)
    pallas_call x1, Pallas kernels, per_device(): pl.pallas_call(functools.partial(fused, ctx, chans), out_shape=jax.ShapeD...  35.1 us
    unnamed x1, local copies, waits for them, and re-layouts  1.67 us

profile of v2, /device:TPU:3, one launch (start us, length us, event | category | flops | bytes accessed | tf_op | source)
XLA Modules:
  0.0 36.7 jit_solution(12537953264107363376)
XLA Ops:
  0.0 35.1 %fused.1 = bf16[128,1024]{1,0:T(8,128)(2,1)} custom-call(bf16[3,128,1024]{2,1,0:T(8,128)(2,1)} %proj_in.1, bf16[3,64,128]{2,1,0:T(8,128)(2,1)} %taps_in.1, f32[16,128]{1,0:T(8,128)} %bitcast.3, f32[16,128]{1,0:T(8,128)} %bitcast.4, f32[1,128]{1,0:T(1,128)} %bitcast.5, bf16[1024,1024]{1,0:T(8,128)(2,1)} %weight_ref.1), custom_call_target="tpu_custom_call" | custom-call | tf_op jit(solution)/shard_map/fused/pallas_call | solution.py:371
  35.1 1.7 %copy.8 = bf16[128,1024]{1,0:T(8,128)(2,1)} copy(bf16[128,1024]{1,0:T(8,128)(2,1)} %fused.1) | data formatting | bytes 524288

commit v3 on v2

--- a/solution.py
+++ b/solution.py
@@ -130,7 +130,7 @@
     flip = one_hot(
         iota((BLOCK, 2 * BLOCK), 1) == BLOCK - iota((BLOCK, 2 * BLOCK), 0), jnp.bfloat16
     )
-    for stream in range(3):
+    def make_bands(stream):
         own = jnp.dot(pick, taps_ref[stream], preferred_element_type=jnp.float32)
         rows = jnp.dot(own.astype(jnp.bfloat16), flip, preferred_element_type=jnp.float32)
         for g in range(groups):
@@ -139,8 +139,9 @@
                 jnp.bfloat16
             )
 
-    for load in loads[1:4]:
-        load.wait()
+    make_bands(1)
+    make_bands(2)
+    loads[1].wait()
     high = modes * groups
     expand = one_hot(iota((high, modes), 0) // groups == iota((high, modes), 1))
     kept = iota((high, width), 1) // GROUP == iota((high, width), 0) % groups
@@ -162,13 +163,6 @@
         )
 
     rate_s[...] = spread_rows(rate_ref[...])
-    residue_s[...] = spread_rows(residue_ref[...]) * jnp.sqrt(2.0 * rate_s[...] / modes)
-    skip_rows = jnp.where(
-        iota((groups, width), 1) // GROUP == iota((groups, width), 0),
-        jnp.broadcast_to(skip_ref[...], (groups, width)),
-        0.0,
-    )
-    skip = jnp.dot(skip_rows, spread, precision=HIGHEST, preferred_element_type=jnp.float32)
 
     def of_mode(ref, m):
         return ref[m * groups : (m + 1) * groups, :]
@@ -233,8 +227,21 @@
         def _():
             end_copies[hop - 1].start()
 
+    make_bands(0)
     for g in range(groups):
         query[pl.ds(g, BLOCK, stride=groups), :] = short(0, g)
+    loads[2].wait()
+    loads[3].wait()
+    residue_s[...] = spread_rows(residue_ref[...]) * jnp.sqrt(2.0 * rate_s[...] / modes)
+    skip_rows = jnp.where(
+        iota((groups, width), 1) // GROUP == iota((groups, width), 0),
+        jnp.broadcast_to(skip_ref[...], (groups, width)),
+        0.0,
+    )
+    skip = jnp.dot(skip_rows, spread, precision=HIGHEST, preferred_element_type=jnp.float32)
+    at_tokens = at.astype(jnp.float32) * float(BLOCK)
+    across = [jnp.exp(of_mode(rate_s, m) * (-float(tokens))) for m in range(modes)]
+    shift = [jnp.exp(-of_mode(rate_s, m) * at_tokens) for m in range(modes)]
 
     for hop in range(1, ctx):
 
@@ -246,21 +253,18 @@
         def _():
             ends[hop - 1] = jnp.zeros((high, lanes), jnp.float32)
 
-    at_tokens = at.astype(jnp.float32) * float(BLOCK)
     entry, weight = [], []
     for m in range(modes):
-        rate = of_mode(rate_s, m)
-        per_device = jnp.exp(rate * (-float(tokens)))
         incoming = jnp.zeros_like(zero)
         for hop in range(ctx - 1, 0, -1):
-            incoming = per_device * incoming + ends[hop - 1, m * groups : (m + 1) * groups, :]
+            incoming = across[m] * incoming + ends[hop - 1, m * groups : (m + 1) * groups, :]
         incoming = jnp.where(at == blocks - 1, incoming, 0.0)
         hop = 1
         while hop < blocks:
             incoming = incoming + pltpu.roll(incoming, GROUP * hop, 1)
             hop *= 2
         own = jnp.where(at >= 1, pltpu.roll(of_mode(state, m), GROUP, 1), 0.0)
-        entry.append(own + jnp.exp(-rate * at_tokens) * incoming)
+        entry.append(own + shift[m] * incoming)
         weight.append(of_mode(residue_s, m))
 
     def step(r, states):

time: 36.9 us -> 37.1 us (level)
  no operation moved by 1% of the time
where the time goes in v3:
time: 37.1 us; the launch traced here: 37 us
  Pallas kernels  35.3 us (95%)
  local copies, waits for them, and re-layouts  1.67 us (5%)
    pallas_call x1, Pallas kernels, per_device(): pl.pallas_call(functools.partial(fused, ctx, chans), out_shape=jax.ShapeD...  35.3 us
    unnamed x1, local copies, waits for them, and re-layouts  1.67 us

profile of v3, /device:TPU:3, one launch (start us, length us, event | category | flops | bytes accessed | tf_op | source)
XLA Modules:
  0.0 37.0 jit_solution(4860539613606209779)
XLA Ops:
  0.0 35.3 %fused.1 = bf16[128,1024]{1,0:T(8,128)(2,1)} custom-call(bf16[3,128,1024]{2,1,0:T(8,128)(2,1)} %proj_in.1, bf16[3,64,128]{2,1,0:T(8,128)(2,1)} %taps_in.1, f32[16,128]{1,0:T(8,128)} %bitcast.3, f32[16,128]{1,0:T(8,128)} %bitcast.4, f32[1,128]{1,0:T(1,128)} %bitcast.5, bf16[1024,1024]{1,0:T(8,128)(2,1)} %weight_ref.1), custom_call_target="tpu_custom_call" | custom-call | tf_op jit(solution)/shard_map/fused/pallas_call | solution.py:375
  35.3 1.7 %copy.8 = bf16[128,1024]{1,0:T(8,128)(2,1)} copy(bf16[128,1024]{1,0:T(8,128)(2,1)} %fused.1) | data formatting | bytes 524288

commit v4 on v3

--- a/solution.py
+++ b/solution.py
@@ -374,7 +374,7 @@
     table = pltpu.VMEM((modes * groups, lanes), jnp.float32)
     return pl.pallas_call(
         functools.partial(fused, ctx, chans),
-        out_shape=jax.ShapeDtypeStruct((width, tokens), jnp.bfloat16),
+        out_shape=pltpu.VMEM((width, tokens), jnp.bfloat16),
         in_specs=[pl.BlockSpec(memory_space=pltpu.HBM)] * 6,
         out_specs=vmem,
         scratch_shapes=[

time: 37.1 us -> 35.4 us (0.954)
  local copies, waits for them, and re-layouts: 1.67 us -> 0.71 us
  Pallas kernels: 35.3 us -> 34.6 us
    unnamed x1, local copies, waits for them, and re-layouts: 1.67 us -> 0.71 us
    pallas_call x1, Pallas kernels: 35.3 us -> 34.6 us  [per_device(): pl.pallas_call(functools.partial(fused, ctx, chans), out_shape=pltpu.VMEM...]
where the time goes in v4:
time: 35.4 us; the launch traced here: 35.3 us
  Pallas kernels  34.6 us (98%)
  local copies, waits for them, and re-layouts  0.71 us (2%)
    pallas_call x1, Pallas kernels, per_device(): pl.pallas_call(functools.partial(fused, ctx, chans), out_shape=pltpu.VMEM...  34.6 us

profile of v4, /device:TPU:3, one launch (start us, length us, event | category | flops | bytes accessed | tf_op | source)
XLA Modules:
  0.0 35.3 jit_solution(12042679496209790120)
XLA Ops:
  0.0 34.6 %fused.1 = bf16[128,1024]{1,0:T(8,128)(2,1)S(1)} custom-call(bf16[3,128,1024]{2,1,0:T(8,128)(2,1)} %proj_in.1, bf16[3,64,128]{2,1,0:T(8,128)(2,1)} %taps_in.1, f32[16,128]{1,0:T(8,128)} %bitcast.3, f32[16,128]{1,0:T(8,128)} %bitcast.4, f32[1,128]{1,0:T(1,128)} %bitcast.5, bf16[1024,1024]{1,0:T(8,128)(2,1)} %weight_ref.1), custom_call_target="tpu_custom_call" | custom-call | tf_op jit(solution)/shard_map/fused/pallas_call | solution.py:375
  34.6 0.7 %copy.8 = bf16[128,1024]{1,0:T(8,128)(2,1)} copy(bf16[128,1024]{1,0:T(8,128)(2,1)S(1)} %fused.1) | data formatting | bytes 524288

commit v5 on v4

--- a/solution.py
+++ b/solution.py
@@ -8,7 +8,7 @@
 
 GROUP = 16
 BLOCK = 128
-PIECES = 4
+PIECES = 8
 MESH = pl.DeviceIdType.MESH
 HIGHEST = lax.Precision.HIGHEST
 

time: 35.4 us -> 35.4 us (level)
  no operation moved by 1% of the time
where the time goes in v5:
time: 35.4 us; the launch traced here: 35.3 us
  Pallas kernels  34.6 us (98%)
  local copies, waits for them, and re-layouts  0.71 us (2%)
    pallas_call x1, Pallas kernels, per_device(): pl.pallas_call(functools.partial(fused, ctx, chans), out_shape=pltpu.VMEM...  34.6 us

profile of v5, /device:TPU:3, one launch (start us, length us, event | category | flops | bytes accessed | tf_op | source)
XLA Modules:
  0.0 35.3 jit_solution(5077335807718240520)
XLA Ops:
  0.0 34.6 %fused.1 = bf16[128,1024]{1,0:T(8,128)(2,1)S(1)} custom-call(bf16[3,128,1024]{2,1,0:T(8,128)(2,1)} %proj_in.1, bf16[3,64,128]{2,1,0:T(8,128)(2,1)} %taps_in.1, f32[16,128]{1,0:T(8,128)} %bitcast.3, f32[16,128]{1,0:T(8,128)} %bitcast.4, f32[1,128]{1,0:T(1,128)} %bitcast.5, bf16[1024,1024]{1,0:T(8,128)(2,1)} %weight_ref.1), custom_call_target="tpu_custom_call" | custom-call | tf_op jit(solution)/shard_map/fused/pallas_call | solution.py:375
  34.6 0.7 %copy.8 = bf16[128,1024]{1,0:T(8,128)(2,1)} copy(bf16[128,1024]{1,0:T(8,128)(2,1)S(1)} %fused.1) | data formatting | bytes 524288

commit v6 on v4

--- a/solution.py
+++ b/solution.py
@@ -198,7 +198,7 @@
         return tuple(d * s + x for d, s in zip(decay, states))
 
     zero = jnp.zeros((groups, lanes), jnp.float32)
-    last = lax.fori_loop(0, BLOCK, gather_step, (zero,) * modes, unroll=8)
+    last = lax.fori_loop(0, BLOCK, gather_step, (zero,) * modes, unroll=16)
     at = iota(zero.shape, 1) // GROUP
     for m in range(modes):
         total, hop = last[m], 1
@@ -279,10 +279,10 @@
         work[where, :] = query[where, :] * parts[0]
         return new
 
-    lax.fori_loop(0, BLOCK, step, tuple(entry), unroll=4)
+    lax.fori_loop(0, BLOCK, step, tuple(entry), unroll=8)
     per_piece = blocks // PIECES
     for g in range(groups):
-        turned = work[pl.ds(g, BLOCK, stride=groups), :].T.astype(jnp.bfloat16)
+        turned = work[pl.ds(g, BLOCK, stride=groups), :].astype(jnp.bfloat16).T
         for b in range(blocks):
             inside = (b % per_piece) * BLOCK
             gath[

time: 35.4 us -> 35.3 us (level)
  no operation moved by 1% of the time
where the time goes in v6:
time: 35.3 us; the launch traced here: 35.1 us
  Pallas kernels  34.4 us (97%)
  local copies, waits for them, and re-layouts  0.71 us (2%)
    pallas_call x1, Pallas kernels, per_device(): pl.pallas_call(functools.partial(fused, ctx, chans), out_shape=pltpu.VMEM...  34.4 us

profile of v6, /device:TPU:3, one launch (start us, length us, event | category | flops | bytes accessed | tf_op | source)
XLA Modules:
  0.0 35.1 jit_solution(702399784101458206)
XLA Ops:
  0.0 34.4 %fused.1 = bf16[128,1024]{1,0:T(8,128)(2,1)S(1)} custom-call(bf16[3,128,1024]{2,1,0:T(8,128)(2,1)} %proj_in.1, bf16[3,64,128]{2,1,0:T(8,128)(2,1)} %taps_in.1, f32[16,128]{1,0:T(8,128)} %bitcast.3, f32[16,128]{1,0:T(8,128)} %bitcast.4, f32[1,128]{1,0:T(1,128)} %bitcast.5, bf16[1024,1024]{1,0:T(8,128)(2,1)} %weight_ref.1), custom_call_target="tpu_custom_call" | custom-call | tf_op jit(solution)/shard_map/fused/pallas_call | solution.py:375
  34.4 0.7 %copy.8 = bf16[128,1024]{1,0:T(8,128)(2,1)} copy(bf16[128,1024]{1,0:T(8,128)(2,1)S(1)} %fused.1) | data formatting | bytes 524288
